TPU v7x, 256 devices: a whole 4x4x8 slice. The times are simulated.
256 devices in a mesh: shard: 32 (over x, z_hi, y), rep: 8 (over z_lo, core).
Axes of the slice: x: 4, y: 4, z: 8 (z_hi: 2, z_lo: 4; z = z_hi * 4 + z_lo), core: 2. Of those that a mesh axis runs over, the one named last changes fastest.
Arguments:
- momentum: bfloat16 [32, 512, 2048], P(None, 'shard'), may hold values from -6 to 6
- gradient: bfloat16 [32, 512, 2048], P(None, 'shard'), may hold values from -6 to 6
Outputs:
- new_momentum: bfloat16 [32, 512, 2048], P(None, 'shard')
- update: bfloat16 [32, 512, 2048], P(None, 'shard')
All inputs are finite; a program needn't handle non-finite values.
Results may differ from a plain program's by a relative error of at most 0.00065.
The roundings to bfloat16 on the way count: a program that leaves them out, or rounds other values in their place, can miss the bound.
Values may be sent and summed in bfloat16 or wider, within the bound.
A program may use at most 64 MiB of HBM per device.

v0:
```python
import jax
import jax.numpy as jnp
from jax import lax
from jax.sharding import PartitionSpec as P

ROWS = 512
COLS = 2048
ITERS = 5
coef_a = 3.4445
coef_b = -4.775
coef_c = 2.0315


def gram_sum(values):
    local_gram = jnp.dot(
        values, values.T, precision=lax.Precision.HIGHEST, preferred_element_type=jnp.float32
    )
    return lax.psum(local_gram, "rep")


def newton_step(gram_matrix, iterate):
    polynomial = coef_b * gram_matrix + coef_c * jnp.dot(
        gram_matrix, gram_matrix, precision=lax.Precision.HIGHEST
    )
    return coef_a * iterate + jnp.dot(polynomial, iterate, precision=lax.Precision.HIGHEST)


def shards(momentum, gradient):
    new_momentum = (0.95 * momentum.astype(jnp.float32) + gradient.astype(jnp.float32)).astype(
        jnp.bfloat16
    )
    blended = (gradient.astype(jnp.float32) + 0.95 * new_momentum.astype(jnp.float32)).astype(
        jnp.bfloat16
    )
    col_width = blended.shape[2] // lax.axis_size("rep")
    col_start = lax.axis_index("rep") * col_width
    col_block = lax.dynamic_slice_in_dim(blended, col_start, col_width, 2)
    regrouped = lax.all_to_all(col_block, "shard", split_axis=0, concat_axis=1, tiled=True)
    scale_value = jnp.sqrt(jnp.float32(max(ROWS, COLS)))
    columns_block = regrouped[0].astype(jnp.float32)
    square_total = lax.psum(jnp.sum(columns_block * columns_block), "rep")
    norm_value = jnp.sqrt(square_total) + 1e-07
    iterate = columns_block / norm_value
    gram_matrix = gram_sum(iterate)
    for sweep in range(ITERS):
        if sweep > 0:
            gram_matrix = gram_sum(iterate)
        iterate = newton_step(gram_matrix, iterate)
    result = (iterate * scale_value).astype(jnp.bfloat16)[None]
    full_matrix = lax.all_gather(result, "rep", axis=2, tiled=True)
    update = lax.all_to_all(full_matrix, "shard", split_axis=1, concat_axis=0, tiled=True)
    return (new_momentum, update)


def solution(mesh):
    return jax.shard_map(
        shards,
        mesh=mesh,
        in_specs=(P(None, "shard", None), P(None, "shard", None)),
        out_specs=(P(None, "shard", None), P(None, "shard", None)),
        check_vma=False,
    )
```

profile of v0, /device:TPU:1, one launch (start us, length us, event | category | flops | bytes accessed | tf_op | source)
XLA Modules:
  0.0 596.6 jit_solution(5018397277071204557)
XLA Ops:
  7.2 0.0 all-reduce.6.cloned.1.call-start
  7.2 0.0 copy-start
  7.2 0.0 copy-start.2
  7.2 4.2 convert_element_type.28
  11.4 0.0 copy-done
  11.4 0.0 copy-done.2
  11.4 1.0 add_convert_fusion
  12.4 0.0 copy-start.1
  12.4 1.6 fusion.8
  14.0 26.4 %all_to_all.21 = bf16[32,16,256]{2,1,0:T(8,128)(2,1)S(1)} all-to-all(bf16[32,16,256]{2,1,0:T(8,128)(2,1)S(1)} %fusion.8), channel_id=1, replica_groups=mesh['shard'=32,'rep'=8] {'shard'}, dimensions={0} | all-to-all | bytes 524288 | tf_op jit(solution)/shard_map/all_to_all | solution.py:38
  40.4 0.7 fusion.7
  41.1 15.6 %psum.42 = f32[]{:T(128)} all-reduce(f32[]{:T(128)} %fusion.7), channel_id=1, replica_groups=mesh['shard'=32,'rep'=8] {'rep'}, use_global_device_ids=true, to_apply=%region_1.0 | all-reduce | flops 1 | bytes 8 | tf_op jit(solution)/shard_map/psum | solution.py:41
  57.4 0.0 copy-done.1
  57.4 0.1 convert_divide_fusion
  57.5 2.0 fusion.9
  59.5 0.0 all-reduce.6.cloned.1.call-update
  59.5 0.0 all-reduce.8.cloned.1.call-start
  59.6 64.8 %all-reduce.6.cloned.1.call-done = f32[512,512]{1,0:T(8,128)} async-done(((f32[512,512]{1,0:T(8,128)}), f32[512,512]{1,0:T(8,128)}) %all-reduce.6.cloned.1.call-update) | async-done | bytes 1048592 | tf_op jit(solution)/shard_map/psum | solution.py:18
  124.4 3.9 fusion.4
  128.4 1.0 convolution_add_fusion.4
  129.4 2.0 fusion.10
  131.4 0.0 all-reduce.8.cloned.1.call-update
  131.4 0.0 all-reduce.10.cloned.1.call-start
  131.4 73.5 %all-reduce.8.cloned.1.call-done = f32[512,512]{1,0:T(8,128)} async-done(((f32[512,512]{1,0:T(8,128)}), f32[512,512]{1,0:T(8,128)}) %all-reduce.8.cloned.1.call-update) | async-done | bytes 1048592 | tf_op jit(solution)/shard_map/psum | solution.py:18
  204.9 3.9 fusion.3
  208.8 1.0 convolution_add_fusion.3
  209.8 2.0 fusion.11
  211.8 0.0 all-reduce.10.cloned.1.call-update
  211.8 0.2 all-reduce.12.cloned.1.call-start
  212.1 73.3 %all-reduce.10.cloned.1.call-done = f32[512,512]{1,0:T(8,128)} async-done(((f32[512,512]{1,0:T(8,128)}), f32[512,512]{1,0:T(8,128)}) %all-reduce.10.cloned.1.call-update) | async-done | bytes 1048592 | tf_op jit(solution)/shard_map/psum | solution.py:18
  285.4 3.9 fusion.2
  289.3 1.0 convolution_add_fusion.2
  290.3 2.0 fusion.12
  292.3 0.0 all-reduce.12.cloned.1.call-update
  292.3 0.0 all-reduce.14.cloned.1.call-start
  292.4 73.5 %all-reduce.12.cloned.1.call-done = f32[512,512]{1,0:T(8,128)} async-done(((f32[512,512]{1,0:T(8,128)}), f32[512,512]{1,0:T(8,128)}) %all-reduce.12.cloned.1.call-update) | async-done | bytes 1048592 | tf_op jit(solution)/shard_map/psum | solution.py:18
  365.9 3.9 fusion.1
  369.8 1.0 convolution_add_fusion.1
  370.8 2.0 fusion.13
  372.8 0.0 all-reduce.14.cloned.1.call-update
  372.8 0.3 all-gather.3.cloned.1.call-start
  373.1 73.2 %all-reduce.14.cloned.1.call-done = f32[512,512]{1,0:T(8,128)} async-done(((f32[512,512]{1,0:T(8,128)}), f32[512,512]{1,0:T(8,128)}) %all-reduce.14.cloned.1.call-update) | async-done | bytes 1048592 | tf_op jit(solution)/shard_map/psum | solution.py:18
  446.3 3.9 fusion
  450.3 1.7 fusion.6
  452.0 0.0 all-gather.3.cloned.1.call-update
  452.0 40.6 %all-gather.3.cloned.1.call-done = bf16[512,2048]{1,0:T(8,128)(2,1)} async-done(((bf16[512,256]{1,0:T(8,128)(2,1)}), bf16[512,2048]{1,0:T(8,128)(2,1)}) %all-gather.3.cloned.1.call-update) | async-done | bytes 2097168 | tf_op jit(solution)/shard_map/all_gather | solution.py:50
  492.6 6.7 %copy.8 = bf16[1,512,2048]{2,0,1:T(2,128)(2,1)} copy(bf16[1,512,2048]{2,1,0:T(8,128)(2,1)} %bitcast.41) | data formatting | bytes 4194304 | tf_op jit(solution)/shard_map/all_gather | solution.py:50
  499.3 0.5 broadcast.39
  499.9 13.2 %reduce.3 = bf16[512,2048]{1,0:T(8,128)(2,1)S(1)} reduce(bf16[512,1,2048]{2,1,0:T(2,128)(2,1)} %bitcast.37, bf16[]{:T(256)} %broadcast.39), dimensions={1}, to_apply=%bitcast.36.reduce_sub_computation | reduce | bytes 4194306
  513.0 2.8 reshape.22
  515.8 62.4 %all_to_all.22 = bf16[32,2,16384]{2,1,0:T(2,128)(2,1)S(1)} all-to-all(bf16[32,2,16384]{2,1,0:T(2,128)(2,1)} %reshape.22), channel_id=1, replica_groups=mesh['shard'=32,'rep'=8] {'shard'}, dimensions={0} | all-to-all | bytes 4194304 | tf_op jit(solution)/shard_map/all_to_all | solution.py:51
  578.2 6.8 %reshape.23 = bf16[512,1,2048]{2,1,0:T(2,128)(2,1)} reshape(bf16[32,2,16384]{2,1,0:T(2,128)(2,1)S(1)} %all_to_all.22) | data formatting | bytes 4194304
  585.0 4.8 copy.6
Async XLA Ops:
  7.2 117.3 %all-reduce.6.cloned.1.call-start = ((), (), s32[]{:S(2)}) async-start(), calls=%async_computation.2 | async-start | bytes 2097152 | tf_op jit(solution)/shard_map/psum | solution.py:18
  7.2 4.2 copy-start
  7.2 4.2 copy-start.2
  12.4 45.0 %copy-start.1 = (bf16[32,16,2048]{2,1,0:T(8,128)(2,1)}, bf16[32,16,2048]{2,1,0:T(8,128)(2,1)S(1)}, u32[]{:S(2)}) copy-start(bf16[32,16,2048]{2,1,0:T(8,128)(2,1)S(1)} %add_convert_fusion) | copy-start | bytes 6291460
  59.5 145.3 %all-reduce.8.cloned.1.call-start = ((), (), s32[]{:S(2)}) async-start(), calls=%async_computation.3 | async-start | bytes 2097152 | tf_op jit(solution)/shard_map/psum | solution.py:18
  131.4 154.0 %all-reduce.10.cloned.1.call-start = ((), (), s32[]{:S(2)}) async-start(), calls=%async_computation.4 | async-start | bytes 2097152 | tf_op jit(solution)/shard_map/psum | solution.py:18
  211.8 154.0 %all-reduce.12.cloned.1.call-start = ((), (), s32[]{:S(2)}) async-start(), calls=%async_computation.5 | async-start | bytes 2097152 | tf_op jit(solution)/shard_map/psum | solution.py:18
  292.3 154.0 %all-reduce.14.cloned.1.call-start = ((), (), s32[]{:S(2)}) async-start(), calls=%async_computation.6 | async-start | bytes 2097152 | tf_op jit(solution)/shard_map/psum | solution.py:18
  372.8 119.8 %all-gather.3.cloned.1.call-start = ((), (), s32[]{:S(2)}) async-start(), calls=%async_computation.7 | async-start | bytes 2359296 | tf_op jit(solution)/shard_map/all_gather | solution.py:50
Sparse Core Ops, SparseCore 0:
  59.7 64.7 all-reduce.5
  131.5 73.3 all-reduce.7
  212.0 73.3 all-reduce.9
  292.4 73.3 all-reduce.11
  373.0 73.3 all-reduce.13
  452.1 40.4 all-gather.2
where the time goes:
time: 597 us
  waiting for transfers between devices  399 us (67%)
  blocking collectives  104 us (17%)
  matrix products  35.3 us (6%)
  local copies, waits for them, and re-layouts  21.6 us (4%)
  other arithmetic  20.7 us (3%)
  between operations  14.9 us (2%)
    psum x5, waiting for transfers between devices, gram_sum(): return lax.psum(local_gram, 'rep')  358 us
    all_to_all x1, blocking collectives, shards(): lax.all_to_all(full_matrix, 'shard', split_axis=1, concat_axis=0, tiled=T...  62.4 us
    all_gather x1, waiting for transfers between devices, shards(): full_matrix = lax.all_gather(result, 'rep', axis=2, tiled=True)  40.6 us
    all_to_all x1, blocking collectives, shards(): lax.all_to_all(col_block, 'shard', split_axis=0, concat_axis=1, tiled=True)  26.4 us
    dot_general x5, matrix products, newton_step(): jnp.dot(gram_matrix, gram_matrix, precision=lax.Precision.HIGHEST)  19.6 us
    psum x1, blocking collectives, shards(): square_total = lax.psum(jnp.sum(columns_block * columns_block), 'rep')  15.6 us
    unnamed x10, local copies, waits for them, and re-layouts  14.8 us
    unnamed x1, other arithmetic  13.2 us
  transfers between devices with their start and end apart: 6, of which 6 were waited for; matrix products, arithmetic and copies ran while one was open for 0% of the time, Pallas kernels for 0%

commit v1 on v0

--- a/solution.py
+++ b/solution.py
@@ -15,7 +15,7 @@
     local_gram = jnp.dot(
         values, values.T, precision=lax.Precision.HIGHEST, preferred_element_type=jnp.float32
     )
-    return lax.psum(local_gram, "rep")
+    return jnp.sum(lax.all_gather(local_gram, "rep"), axis=0)
 
 
 def newton_step(gram_matrix, iterate):

time: 597 us -> 706 us (1.18)
  waiting for transfers between devices: 399 us -> 494 us
  other arithmetic: 20.7 us -> 43.9 us
  matrix products: 35.3 us -> 25.1 us
    all_gather x0 -> x5, waiting for transfers between devices: none -> 455 us  [gram_sum(): return jnp.sum(lax.all_gather(local_gram, 'rep'), axis=0)]
    psum x5 -> x0, waiting for transfers between devices: 358 us -> none  [gram_sum(): return lax.psum(local_gram, 'rep')]
    reduce_sum x0 -> x5, other arithmetic: none -> 22.5 us  [gram_sum(): return jnp.sum(lax.all_gather(local_gram, 'rep'), axis=0)]
    dot_general x5, matrix products: 19.6 us -> 9.4 us  [newton_step(): jnp.dot(gram_matrix, gram_matrix, precision=lax.Precision.HIGHEST)]
    unnamed x10 -> x8, local copies, waits for them, and re-layouts: 14.8 us -> 14.8 us
where the time goes in v1:
time: 706 us; the launch traced here: 705 us
  waiting for transfers between devices  494 us (70%)
  blocking collectives  104 us (15%)
  other arithmetic  43.9 us (6%)
  matrix products  25.1 us (4%)
  local copies, waits for them, and re-layouts  21.6 us (3%)
  between operations  14.9 us (2%)
    all_gather x5, waiting for transfers between devices, gram_sum(): return jnp.sum(lax.all_gather(local_gram, 'rep'), axis=0)  455 us
    all_to_all x1, blocking collectives, shards(): lax.all_to_all(full_matrix, 'shard', split_axis=1, concat_axis=0, tiled=T...  62.4 us
    all_gather x1, waiting for transfers between devices, shards(): full_matrix = lax.all_gather(result, 'rep', axis=2, tiled=True)  39.8 us
    all_to_all x1, blocking collectives, shards(): lax.all_to_all(col_block, 'shard', split_axis=0, concat_axis=1, tiled=True)  26.4 us
    reduce_sum x5, other arithmetic, gram_sum(): return jnp.sum(lax.all_gather(local_gram, 'rep'), axis=0)  22.5 us
    psum x1, blocking collectives, shards(): square_total = lax.psum(jnp.sum(columns_block * columns_block), 'rep')  15.6 us
    unnamed x8, local copies, waits for them, and re-layouts  14.8 us
  transfers between devices with their start and end apart: 6, of which 6 were waited for; matrix products, arithmetic and copies ran while one was open for 0% of the time, Pallas kernels for 0%

profile of v1, /device:TPU:1, one launch (start us, length us, event | category | flops | bytes accessed | tf_op | source)
XLA Modules:
  0.0 705.1 jit_solution(12453261164874953601)
XLA Ops:
  7.2 0.0 copy-start
  7.2 0.0 all-gather.13.cloned.1.call-start
  7.2 0.0 copy-start.1
  7.2 4.2 convert_element_type.28
  11.4 0.0 copy-done
  11.4 0.0 copy-done.1
  11.4 2.1 add_convert_fusion
  13.6 1.2 fusion.8
  14.8 26.4 %all_to_all.21 = bf16[32,16,256]{2,1,0:T(8,128)(2,1)S(1)} all-to-all(bf16[32,16,256]{2,1,0:T(8,128)(2,1)S(1)} %fusion.8), channel_id=1, replica_groups=mesh['shard'=32,'rep'=8] {'shard'}, dimensions={0} | all-to-all | bytes 524288 | tf_op jit(solution)/shard_map/all_to_all | solution.py:38
  41.2 0.7 fusion.7
  41.9 15.6 %psum.7 = f32[]{:T(128)} all-reduce(f32[]{:T(128)} %fusion.7), channel_id=1, replica_groups=mesh['shard'=32,'rep'=8] {'rep'}, use_global_device_ids=true, to_apply=%region_1.0 | all-reduce | flops 1 | bytes 8 | tf_op jit(solution)/shard_map/psum | solution.py:41
  58.2 0.1 convert_divide_fusion
  58.3 2.0 fusion.9
  60.3 0.0 all-gather.13.cloned.1.call-update
  60.3 0.0 all-gather.15.cloned.1.call-start
  60.4 84.8 %all-gather.13.cloned.1.call-done = f32[4096,512]{1,0:T(8,128)} async-done(((f32[512,512]{1,0:T(8,128)}), f32[4096,512]{1,0:T(8,128)}) %all-gather.13.cloned.1.call-update) | async-done | bytes 8388624 | tf_op jit(solution)/shard_map/all_gather | solution.py:18
  145.1 4.5 reduce_sum.55
  149.6 1.9 fusion.4
  151.5 1.0 convolution_add_fusion.4
  152.5 2.0 fusion.10
  154.5 0.0 all-gather.15.cloned.1.call-update
  154.6 0.2 all-gather.17.cloned.1.call-start
  154.8 92.4 %all-gather.15.cloned.1.call-done = f32[4096,512]{1,0:T(8,128)} async-done(((f32[512,512]{1,0:T(8,128)}), f32[4096,512]{1,0:T(8,128)}) %all-gather.15.cloned.1.call-update) | async-done | bytes 8388624 | tf_op jit(solution)/shard_map/all_gather | solution.py:18
  247.1 4.5 reduce_sum.56
  251.6 1.9 fusion.3
  253.5 1.0 convolution_add_fusion.3
  254.5 2.0 fusion.11
  256.5 0.0 all-gather.17.cloned.1.call-update
  256.6 0.0 all-gather.19.cloned.1.call-start
  256.6 92.5 %all-gather.17.cloned.1.call-done = f32[4096,512]{1,0:T(8,128)} async-done(((f32[512,512]{1,0:T(8,128)}), f32[4096,512]{1,0:T(8,128)}) %all-gather.17.cloned.1.call-update) | async-done | bytes 8388624 | tf_op jit(solution)/shard_map/all_gather | solution.py:18
  349.2 4.5 reduce_sum.57
  353.6 1.9 fusion.2
  355.5 1.0 convolution_add_fusion.2
  356.5 2.0 fusion.12
  358.5 0.0 all-gather.19.cloned.1.call-update
  358.6 0.0 all-gather.21.cloned.1.call-start
  358.6 92.5 %all-gather.19.cloned.1.call-done = f32[4096,512]{1,0:T(8,128)} async-done(((f32[512,512]{1,0:T(8,128)}), f32[4096,512]{1,0:T(8,128)}) %all-gather.19.cloned.1.call-update) | async-done | bytes 8388624 | tf_op jit(solution)/shard_map/all_gather | solution.py:18
  451.2 4.5 reduce_sum.58
  455.6 1.9 fusion.1
  457.5 1.0 convolution_add_fusion.1
  458.5 2.0 fusion.13
  460.5 0.0 all-gather.21.cloned.1.call-update
  460.6 0.3 all-gather.23.cloned.1.call-start
  460.8 92.3 %all-gather.21.cloned.1.call-done = f32[4096,512]{1,0:T(8,128)} async-done(((f32[512,512]{1,0:T(8,128)}), f32[4096,512]{1,0:T(8,128)}) %all-gather.21.cloned.1.call-update) | async-done | bytes 8388624 | tf_op jit(solution)/shard_map/all_gather | solution.py:18
  553.2 4.5 reduce_sum.59
  557.7 1.9 fusion
  559.5 1.7 fusion.6
  561.2 0.0 all-gather.23.cloned.1.call-update
  561.3 39.8 %all-gather.23.cloned.1.call-done = bf16[512,2048]{1,0:T(8,128)(2,1)} async-done(((bf16[512,256]{1,0:T(8,128)(2,1)}), bf16[512,2048]{1,0:T(8,128)(2,1)}) %all-gather.23.cloned.1.call-update) | async-done | bytes 2097168 | tf_op jit(solution)/shard_map/all_gather | solution.py:50
  601.1 6.7 copy.8
  607.9 0.5 broadcast.39
  608.4 13.2 %reduce.3 = bf16[512,2048]{1,0:T(8,128)(2,1)S(1)} reduce(bf16[512,1,2048]{2,1,0:T(2,128)(2,1)} %bitcast.42, bf16[]{:T(256)} %broadcast.39), dimensions={1}, to_apply=%bitcast.41.reduce_sub_computation | reduce | bytes 4194306
  621.5 2.8 reshape.27
  624.3 62.4 %all_to_all.22 = bf16[32,2,16384]{2,1,0:T(2,128)(2,1)S(1)} all-to-all(bf16[32,2,16384]{2,1,0:T(2,128)(2,1)} %reshape.27), channel_id=1, replica_groups=mesh['shard'=32,'rep'=8] {'shard'}, dimensions={0} | all-to-all | bytes 4194304 | tf_op jit(solution)/shard_map/all_to_all | solution.py:51
  686.7 6.8 reshape.28
  693.5 4.8 copy.6
Async XLA Ops:
  7.2 4.3 copy-start
  7.2 138.0 %all-gather.13.cloned.1.call-start = ((), (), s32[]{:S(2)}) async-start(), calls=%async_computation.2 | async-start | bytes 9437184 | tf_op jit(solution)/shard_map/all_gather | solution.py:18
  7.2 4.2 copy-start.1
  60.3 186.8 %all-gather.15.cloned.1.call-start = ((), (), s32[]{:S(2)}) async-start(), calls=%async_computation.3 | async-start | bytes 9437184 | tf_op jit(solution)/shard_map/all_gather | solution.py:18
  154.6 194.6 %all-gather.17.cloned.1.call-start = ((), (), s32[]{:S(2)}) async-start(), calls=%async_computation.4 | async-start | bytes 9437184 | tf_op jit(solution)/shard_map/all_gather | solution.py:18
  256.6 194.6 %all-gather.19.cloned.1.call-start = ((), (), s32[]{:S(2)}) async-start(), calls=%async_computation.5 | async-start | bytes 9437184 | tf_op jit(solution)/shard_map/all_gather | solution.py:18
  358.6 194.6 %all-gather.21.cloned.1.call-start = ((), (), s32[]{:S(2)}) async-start(), calls=%async_computation.6 | async-start | bytes 9437184 | tf_op jit(solution)/shard_map/all_gather | solution.py:18
  460.6 140.5 %all-gather.23.cloned.1.call-start = ((), (), s32[]{:S(2)}) async-start(), calls=%async_computation.7 | async-start | bytes 2359296 | tf_op jit(solution)/shard_map/all_gather | solution.py:50
Sparse Core Ops, SparseCore 0:
  60.5 84.6 all-gather.12
  154.7 92.4 all-gather.14
  256.7 92.4 all-gather.16
  358.7 92.4 all-gather.18
  460.7 92.4 all-gather.20
  561.4 39.6 all-gather.22

commit v2 on v0

--- a/solution.py
+++ b/solution.py
@@ -48,7 +48,12 @@
         iterate = newton_step(gram_matrix, iterate)
     result = (iterate * scale_value).astype(jnp.bfloat16)[None]
     full_matrix = lax.all_gather(result, "rep", axis=2, tiled=True)
-    update = lax.all_to_all(full_matrix, "shard", split_axis=1, concat_axis=0, tiled=True)
+    update = jnp.concatenate(
+        lax.all_to_all(
+            jnp.stack(jnp.split(full_matrix, lax.axis_size("shard"), axis=1)), "shard", 0, 0
+        ),
+        axis=0,
+    )
     return (new_momentum, update)
 
 

time: 597 us -> 578 us (0.968)
  other arithmetic: 20.7 us -> 7.52 us
  local copies, waits for them, and re-layouts: 21.6 us -> 15.1 us
    unnamed x1 -> x0, other arithmetic: 13.2 us -> none
    all_gather x1 -> x0, local copies, waits for them, and re-layouts: 6.75 us -> none  [shards(): full_matrix = lax.all_gather(result, 'rep', axis=2, tiled=True)]
    unnamed x10 -> x40, local copies, waits for them, and re-layouts: 14.8 us -> 15.1 us
where the time goes in v2:
time: 578 us; the launch traced here: 577 us
  waiting for transfers between devices  399 us (69%)
  blocking collectives  104 us (18%)
  matrix products  35.1 us (6%)
  local copies, waits for them, and re-layouts  15.1 us (3%)
  between operations  15.1 us (3%)
  other arithmetic  7.52 us (1%)
    psum x5, waiting for transfers between devices, gram_sum(): return lax.psum(local_gram, 'rep')  359 us
    all_to_all x1, blocking collectives, shards(): lax.all_to_all(jnp.stack(jnp.split(full_matrix, lax.axis_size('shard'), a...  62.2 us
    all_gather x1, waiting for transfers between devices, shards(): full_matrix = lax.all_gather(result, 'rep', axis=2, tiled=True)  40.6 us
    all_to_all x1, blocking collectives, shards(): lax.all_to_all(col_block, 'shard', split_axis=0, concat_axis=1, tiled=True)  26.4 us
    dot_general x5, matrix products, newton_step(): jnp.dot(gram_matrix, gram_matrix, precision=lax.Precision.HIGHEST)  19.4 us
    psum x1, blocking collectives, shards(): square_total = lax.psum(jnp.sum(columns_block * columns_block), 'rep')  15.6 us
    unnamed x40, local copies, waits for them, and re-layouts  15.1 us
  transfers between devices with their start and end apart: 6, of which 6 were waited for; matrix products, arithmetic and copies ran while one was open for 0% of the time, Pallas kernels for 0%

profile of v2, /device:TPU:1, one launch (start us, length us, event | category | flops | bytes accessed | tf_op | source)
XLA Modules:
  0.0 576.7 jit_solution(12165367721038447219)
XLA Ops:
  7.2 0.0 all-reduce.6.cloned.1.call-start
  7.2 0.0 copy-start
  7.2 0.0 copy-start.2
  7.2 4.2 convert_element_type.28
  11.4 0.0 copy-done
  11.4 0.0 copy-done.2
  11.4 1.0 add_convert_fusion
  12.4 0.0 copy-start.1
  12.4 1.6 fusion.8
  14.0 26.4 %all_to_all.14 = bf16[32,16,256]{2,1,0:T(8,128)(2,1)S(1)} all-to-all(bf16[32,16,256]{2,1,0:T(8,128)(2,1)S(1)} %fusion.8), channel_id=1, replica_groups=mesh['shard'=32,'rep'=8] {'shard'}, dimensions={0} | all-to-all | bytes 524288 | tf_op jit(solution)/shard_map/all_to_all | solution.py:38
  40.4 0.7 fusion.7
  41.1 15.6 %psum.42 = f32[]{:T(128)} all-reduce(f32[]{:T(128)} %fusion.7), channel_id=1, replica_groups=mesh['shard'=32,'rep'=8] {'rep'}, use_global_device_ids=true, to_apply=%region_1.0 | all-reduce | flops 1 | bytes 8 | tf_op jit(solution)/shard_map/psum | solution.py:41
  57.4 0.1 convert_divide_fusion
  57.5 2.0 fusion.9
  59.5 0.0 copy-done.1
  59.5 0.0 all-reduce.6.cloned.1.call-update
  59.5 0.0 all-reduce.8.cloned.1.call-start
  59.6 64.8 %all-reduce.6.cloned.1.call-done = f32[512,512]{1,0:T(8,128)} async-done(((f32[512,512]{1,0:T(8,128)}), f32[512,512]{1,0:T(8,128)}) %all-reduce.6.cloned.1.call-update) | async-done | bytes 1048592 | tf_op jit(solution)/shard_map/psum | solution.py:18
  124.4 3.9 fusion.4
  128.3 1.0 convolution_add_fusion.4
  129.3 2.0 fusion.10
  131.3 0.0 all-reduce.8.cloned.1.call-update
  131.4 0.0 all-reduce.10.cloned.1.call-start
  131.4 73.5 %all-reduce.8.cloned.1.call-done = f32[512,512]{1,0:T(8,128)} async-done(((f32[512,512]{1,0:T(8,128)}), f32[512,512]{1,0:T(8,128)}) %all-reduce.8.cloned.1.call-update) | async-done | bytes 1048592 | tf_op jit(solution)/shard_map/psum | solution.py:18
  204.9 3.9 fusion.3
  208.8 1.0 convolution_add_fusion.3
  209.8 2.0 fusion.11
  211.8 0.0 all-reduce.10.cloned.1.call-update
  211.8 0.2 all-reduce.12.cloned.1.call-start
  212.0 73.3 %all-reduce.10.cloned.1.call-done = f32[512,512]{1,0:T(8,128)} async-done(((f32[512,512]{1,0:T(8,128)}), f32[512,512]{1,0:T(8,128)}) %all-reduce.10.cloned.1.call-update) | async-done | bytes 1048592 | tf_op jit(solution)/shard_map/psum | solution.py:18
  285.4 3.9 fusion.2
  289.3 1.0 convolution_add_fusion.2
  290.3 2.0 fusion.12
  292.3 0.0 all-reduce.12.cloned.1.call-update
  292.3 0.0 all-reduce.14.cloned.1.call-start
  292.4 73.5 %all-reduce.12.cloned.1.call-done = f32[512,512]{1,0:T(8,128)} async-done(((f32[512,512]{1,0:T(8,128)}), f32[512,512]{1,0:T(8,128)}) %all-reduce.12.cloned.1.call-update) | async-done | bytes 1048592 | tf_op jit(solution)/shard_map/psum | solution.py:18
  365.8 3.9 fusion.1
  369.7 1.0 convolution_add_fusion.1
  370.7 2.0 fusion.13
  372.7 0.0 all-reduce.14.cloned.1.call-update
  372.7 0.0 all-gather.3.cloned.1.call-start
  372.8 73.5 %all-reduce.14.cloned.1.call-done = f32[512,512]{1,0:T(8,128)} async-done(((f32[512,512]{1,0:T(8,128)}), f32[512,512]{1,0:T(8,128)}) %all-reduce.14.cloned.1.call-update) | async-done | bytes 1048592 | tf_op jit(solution)/shard_map/psum | solution.py:18
  446.2 3.9 fusion
  450.1 1.7 fusion.6
  451.8 0.0 all-gather.3.cloned.1.call-update
  451.9 40.6 %all-gather.3.cloned.1.call-done = bf16[512,2048]{1,0:T(8,128)(2,1)} async-done(((bf16[512,256]{1,0:T(8,128)(2,1)}), bf16[512,2048]{1,0:T(8,128)(2,1)}) %all-gather.3.cloned.1.call-update) | async-done | bytes 2097168 | tf_op jit(solution)/shard_map/all_gather | solution.py:50
  492.5 1.0 constant_dynamic-update-slice_fusion.31
  493.5 0.8 constant_dynamic-update-slice_fusion.30
  494.3 0.8 constant_dynamic-update-slice_fusion.29
  495.1 0.8 constant_dynamic-update-slice_fusion.28
  496.0 0.8 constant_dynamic-update-slice_fusion.27
  496.8 0.8 constant_dynamic-update-slice_fusion.26
  497.7 0.8 constant_dynamic-update-slice_fusion.25
  498.5 0.8 constant_dynamic-update-slice_fusion.24
  499.4 0.8 constant_dynamic-update-slice_fusion.23
  500.2 0.8 constant_dynamic-update-slice_fusion.22
  501.1 0.8 constant_dynamic-update-slice_fusion.21
  501.9 0.8 constant_dynamic-update-slice_fusion.20
  502.7 0.8 constant_dynamic-update-slice_fusion.19
  503.6 0.8 constant_dynamic-update-slice_fusion.18
  504.4 0.8 constant_dynamic-update-slice_fusion.17
  505.3 0.8 constant_dynamic-update-slice_fusion.16
  506.4 62.2 %all_to_all.15 = bf16[32,1,16,2048]{3,2,1,0:T(8,128)(2,1)S(1)} all-to-all(bf16[32,1,16,2048]{3,2,1,0:T(8,128)(2,1)S(1)} %constant_dynamic-update-slice_fusion), channel_id=1, replica_groups=mesh['shard'=32,'rep'=8] {'shard'}, dimensions={0} | all-to-all | bytes 4194304 | tf_op jit(solution)/shard_map/all_to_all | solution.py:52
  568.6 1.3 copy.41
  (18 shorter events, 0.1 us)
Async XLA Ops:
  7.2 117.3 %all-reduce.6.cloned.1.call-start = ((), (), s32[]{:S(2)}) async-start(), calls=%async_computation.2 | async-start | bytes 2097152 | tf_op jit(solution)/shard_map/psum | solution.py:18
  7.2 4.2 copy-start
  7.2 4.2 copy-start.2
  12.4 47.1 %copy-start.1 = (bf16[32,16,2048]{2,1,0:T(8,128)(2,1)}, bf16[32,16,2048]{2,1,0:T(8,128)(2,1)S(1)}, u32[]{:S(2)}) copy-start(bf16[32,16,2048]{2,1,0:T(8,128)(2,1)S(1)} %add_convert_fusion) | copy-start | bytes 6291460
  59.5 145.3 %all-reduce.8.cloned.1.call-start = ((), (), s32[]{:S(2)}) async-start(), calls=%async_computation.3 | async-start | bytes 2097152 | tf_op jit(solution)/shard_map/psum | solution.py:18
  131.4 154.0 %all-reduce.10.cloned.1.call-start = ((), (), s32[]{:S(2)}) async-start(), calls=%async_computation.4 | async-start | bytes 2097152 | tf_op jit(solution)/shard_map/psum | solution.py:18
  211.8 154.0 %all-reduce.12.cloned.1.call-start = ((), (), s32[]{:S(2)}) async-start(), calls=%async_computation.5 | async-start | bytes 2097152 | tf_op jit(solution)/shard_map/psum | solution.py:18
  292.3 153.9 %all-reduce.14.cloned.1.call-start = ((), (), s32[]{:S(2)}) async-start(), calls=%async_computation.6 | async-start | bytes 2097152 | tf_op jit(solution)/shard_map/psum | solution.py:18
  372.7 119.7 %all-gather.3.cloned.1.call-start = ((), (), s32[]{:S(2)}) async-start(), calls=%async_computation.7 | async-start | bytes 2359296 | tf_op jit(solution)/shard_map/all_gather | solution.py:50
  492.5 13.7 %copy-start.3 = (bf16[512,2048]{1,0:T(8,128)(2,1)S(1)}, bf16[512,2048]{1,0:T(8,128)(2,1)}, u32[]{:S(2)}) copy-start(bf16[512,2048]{1,0:T(8,128)(2,1)} %all-gather.3.cloned.1.call-done) | copy-start | bytes 6291460
Sparse Core Ops, SparseCore 0:
  59.7 64.7 all-reduce.5
  131.5 73.3 all-reduce.7
  211.9 73.3 all-reduce.9
  292.4 73.3 all-reduce.11
  372.9 73.3 all-reduce.13
  452.0 40.4 all-gather.2
